TPU v7x, 128 devices: a whole 4x4x4 slice. The times are simulated.
128 devices in a mesh: seq: 16 (over x_lo, z, core), tp: 8 (over y, x_hi).
Axes of the slice: x: 4 (x_hi: 2, x_lo: 2; x = x_hi * 2 + x_lo), y: 4, z: 4, core: 2. Of those that a mesh axis runs over, the one named last changes fastest.
Arguments:
- hidden_in: bfloat16 [6144, 3584], P('seq'), may hold values from -48 to 48
- joined_inputs: bfloat16 [6144, 8192], P('seq', 'tp'), may hold values from -64 to 64
- lengths: int32 [4], replicated, may hold values from 1 to 3072, 6144 in all
- o_weight: bfloat16 [4096, 3584], P('tp'), may hold values from -0.09375 to 0.09375
- gate_up: float32 [2, 3584, 7168], P(None, ('seq', 'tp')), may hold values from -0.09375 to 0.09375
- down_weight: bfloat16 [7168, 3584], P('tp'), may hold values from -0.0625 to 0.0625
- next_weight: bfloat16 [3584, 8192], P(None, 'tp'), may hold values from -0.09375 to 0.09375
- post_attn_gain: float32 [3584], replicated, may hold values from 0.1 to 1.9
- pre_ffw_gain: float32 [3584], replicated, may hold values from 0.1 to 1.9
- post_ffw_gain: float32 [3584], replicated, may hold values from 0.1 to 1.9
- next_gain: float32 [3584], replicated, may hold values from 0.1 to 1.9
Outputs:
- next_qkv: bfloat16 [6144, 8192], P('seq', 'tp')
Inputs may be any that keep to these rules, and one draw needn't show every extreme that they name: The lengths of 4 prompts laid end to end; they sum to 6144 and the longest is exactly 3072.
All inputs are finite; a program needn't handle non-finite values.
Results may differ from a plain program's by a relative error of at most 0.022.
Values may be sent and summed in bfloat16 or wider, within the bound.
A program may use at most 192 MiB of HBM per device.

v0:
```python
import jax
import jax.numpy as jnp
from jax import lax
from jax.sharding import PartitionSpec as P

HEADS = 16
KV_HEADS = 8
HEAD_DIM = 256


def rms_norm(values, gain):
    meansq = jnp.mean(values * values, axis=-1, keepdims=True)
    return values * lax.rsqrt(meansq + 1e-06) * gain


def local(
    hidden_in,
    joined_inputs,
    lengths,
    o_weight,
    gate_up,
    down_weight,
    next_weight,
    post_attn_gain,
    pre_ffw_gain,
    post_ffw_gain,
    next_gain,
):
    tp_count = lax.axis_size("tp")
    row_count = hidden_in.shape[0]
    per_group = HEADS // KV_HEADS
    group_cols = (per_group + 2) * HEAD_DIM
    local_groups = joined_inputs.shape[1] // group_cols
    grouped = joined_inputs.reshape(row_count, local_groups, group_cols)
    queries = grouped[:, :, : per_group * HEAD_DIM].reshape(
        row_count, local_groups, per_group, HEAD_DIM
    )
    own_keys = grouped[:, :, per_group * HEAD_DIM : (per_group + 1) * HEAD_DIM]
    own_values = grouped[:, :, (per_group + 1) * HEAD_DIM :]
    keys_all, values_all = (
        lax.all_gather(own_keys, "seq", axis=0, tiled=True),
        lax.all_gather(own_values, "seq", axis=0, tiled=True),
    )
    total_rows = keys_all.shape[0]
    seq_index = lax.axis_index("seq")
    position = seq_index * row_count
    ends = jnp.cumsum(lengths)
    places = jnp.arange(total_rows, dtype=jnp.int32)
    prompt_ids = jnp.sum((places[:, None] >= ends[None, :]).astype(jnp.int32), axis=1)
    query_place = position + jnp.arange(row_count, dtype=jnp.int32)
    query_ids = lax.dynamic_slice_in_dim(prompt_ids, position, row_count, 0)
    scale = HEAD_DIM ** (-0.5)
    scores = (
        jnp.einsum("qgrd,kgd->qgrk", queries, keys_all, preferred_element_type=jnp.float32) * scale
    )
    allowed = (
        (query_ids[:, None] == prompt_ids[None, :]) & (places[None, :] <= query_place[:, None])
    )[:, None, None, :]
    scores = jnp.where(allowed, scores, -jnp.inf)
    peak = jnp.max(scores, axis=-1, keepdims=True)
    weights = jnp.where(allowed, jnp.exp(scores - peak), 0.0)
    norm_sum = jnp.sum(weights, axis=-1)
    blended = jnp.einsum(
        "qgrk,kgd->qgrd",
        weights.astype(jnp.bfloat16),
        values_all,
        preferred_element_type=jnp.float32,
    )
    blended = blended / norm_sum[..., None]
    attended = blended.astype(jnp.bfloat16).reshape(row_count, local_groups * per_group * HEAD_DIM)
    projected = jnp.dot(attended, o_weight, preferred_element_type=jnp.float32)
    tp_index = lax.axis_index("tp")
    slice_rows = row_count // tp_count

    def scattered(values):
        return lax.psum_scatter(
            values.astype(jnp.bfloat16), "tp", scatter_dimension=0, tiled=True
        ).astype(jnp.float32)

    own_hidden = lax.dynamic_slice_in_dim(hidden_in, tp_index * slice_rows, slice_rows, 0)
    residual_mid = own_hidden.astype(jnp.float32) + rms_norm(scattered(projected), post_attn_gain)
    ffw_in = rms_norm(residual_mid, pre_ffw_gain).astype(jnp.bfloat16)
    ffw_in = lax.all_gather(ffw_in, "tp", axis=0, tiled=True)
    server_low = gate_up.astype(jnp.bfloat16)
    unit_rows = lax.all_to_all(server_low, "tp", split_axis=2, concat_axis=1, tiled=True)
    local_units = lax.all_gather(unit_rows, "seq", axis=1, tiled=True)
    gate = jnp.dot(ffw_in, local_units[0], preferred_element_type=jnp.float32)
    up_part = jnp.dot(ffw_in, local_units[1], preferred_element_type=jnp.float32)
    activated = (jax.nn.gelu(gate, approximate=True) * up_part).astype(jnp.bfloat16)
    ffw_out = jnp.dot(activated, down_weight, preferred_element_type=jnp.float32)
    residual_out = residual_mid + rms_norm(scattered(ffw_out), post_ffw_gain)
    next_in = rms_norm(residual_out, next_gain).astype(jnp.bfloat16)
    next_in = lax.all_gather(next_in, "tp", axis=0, tiled=True)
    return jnp.dot(next_in, next_weight, preferred_element_type=jnp.float32).astype(jnp.bfloat16)


def solution(mesh):
    in_specs = (
        P("seq", None),
        P("seq", "tp"),
        P(),
        P("tp", None),
        P(None, ("seq", "tp"), None),
        P("tp", None),
        P(None, "tp"),
        P(),
        P(),
        P(),
        P(),
    )
    out_specs = P("seq", "tp")
    return jax.shard_map(local, mesh=mesh, in_specs=in_specs, out_specs=out_specs, check_vma=False)
```

profile of v0, /device:TPU:1, one launch (start us, length us, event | category | flops | bytes accessed | tf_op | source)
XLA Modules:
  0.0 497.7 jit_solution(12675945497495161882)
XLA Ops:
  6.5 1.8 fusion.47
  8.3 0.0 all-gather.6.cloned.1.call-update
  8.3 0.0 all-gather.8.cloned.1.call-start
  8.4 0.7 all-gather.8.cloned.1.call-update
  9.1 0.0 reduce-scatter.3.cloned.1.call-start
  9.1 1.0 slice.21
  10.2 0.8 reduce-window.8
  11.0 0.2 copy.48
  11.2 0.1 convert_reduce_fusion
  11.4 0.1 dynamic_slice.7
  11.5 3.8 fusion.6
  15.2 33.6 %all-gather.6.cloned.1.call-done = bf16[6144,1,256]{2,0,1:T(8,128)(2,1)} async-done(((bf16[384,1,256]{2,0,1:T(8,128)(2,1)}), bf16[6144,1,256]{2,0,1:T(8,128)(2,1)}) %all-gather.6.cloned.1.call-update) | async-done | bytes 3145744 | tf_op jit(solution)/shard_map/all_gather | solution.py:41
  48.8 5.4 %fusion = (f32[384,2]{0,1:T(2,128)S(1)}, f32[6144,384,2]{1,0,2:T(8,128)S(1)}) fusion(pred[384,6144]{0,1:T(8,128)(4,1)} %fusion.6, bf16[384,2,256]{0,2,1:T(8,128)(2,1)S(1)} %bitcast.100, bf16[6144,1,256]{2,0,1:T(8,128)(2,1)} %all-gather.6.cloned.1.call-done), kind=kOutput, calls=%fused_computation.2 | convolution fusion | flops 2430074112 | bytes 24775680 | tf_op jit(solution)/shard_map/qgrd,kgd->qgrk/dot_general | solution.py:54
  54.2 6.4 %copy-done = f32[6144,384,2]{1,0,2:T(8,128)} copy-done((f32[6144,384,2]{1,0,2:T(8,128)}, f32[6144,384,2]{1,0,2:T(8,128)S(1)}, u32[]{:S(2)}) %copy-start) | copy-done | bytes 18874392
  60.6 6.1 %fusion.1 = f32[384,2]{0,1:T(2,128)S(1)} fusion(f32[6144,384,2]{1,0,2:T(8,128)S(1)} %get-tuple-element.10, f32[384,2]{0,1:T(2,128)S(1)} %get-tuple-element.9, pred[384,6144]{0,1:T(8,128)(4,1)} %fusion.6), kind=kLoop, calls=%fused_computation.3 | loop fusion | flops 23592192 | bytes 21239808 | tf_op jit(solution)/shard_map/reduce_sum | solution.py:62
  66.8 19.7 %all-gather.8.cloned.1.call-done = bf16[6144,1,256]{2,0,1:T(8,128)(2,1)} async-done(((bf16[384,1,256]{2,0,1:T(8,128)(2,1)}), bf16[6144,1,256]{2,0,1:T(8,128)(2,1)}) %all-gather.8.cloned.1.call-update) | async-done | bytes 3145744 | tf_op jit(solution)/shard_map/all_gather | solution.py:42
  86.5 13.2 %fusion.32 = bf16[1,256,384,2]{2,1,3,0:T(8,128)(2,1)S(1)} fusion(bf16[6144,1,256]{2,0,1:T(8,128)(2,1)} %all-gather.8.cloned.1.call-done, f32[6144,384,2]{1,0,2:T(8,128)} %copy-done, f32[384,2]{0,1:T(2,128)S(1)} %get-tuple-element.9, pred[384,6144]{0,1:T(8,128)(4,1)} %fusion.6, f32[384,2]{0,1:T(2,128)S(1)} %fusion.1), kind=kOutput, calls=%fused_computation.33 | convolution fusion | flops 2439905280 | bytes 24778752 | tf_op jit(solution)/shard_map/qgrk,kgd->qgrd/dot_general | solution.py:63
  99.7 3.2 convolution_convert_fusion
  102.8 0.0 reduce-scatter.3.cloned.1.call-update
  102.9 0.2 all-gather.12.cloned.1.call-start
  103.1 0.5 copy.72
  103.6 6.2 %copy.53 = bf16[2,28,7168]{1,0,2:T(2,128)(2,1)} copy(bf16[2,28,7168]{2,1,0:T(8,128)(2,1)S(1)} %copy.72) | data formatting | bytes 1605632 | tf_op jit(solution)/shard_map/convert_element_type | solution.py:84
  109.8 8.3 %reshape.151 = bf16[8,2,25088]{2,1,0:T(2,128)(2,1)S(1)} reshape(bf16[7168,2,28]{2,1,0:T(2,128)(2,1)} %bitcast.95) | data formatting | bytes 1605632
  118.0 21.5 %all_to_all.18 = bf16[8,2,25088]{2,1,0:T(2,128)(2,1)S(1)} all-to-all(bf16[8,2,25088]{2,1,0:T(2,128)(2,1)S(1)} %reshape.151), channel_id=1, replica_groups=mesh['seq'=16,'tp'=8] {'tp'}, dimensions={0} | all-to-all | bytes 1605632 | tf_op jit(solution)/shard_map/all_to_all | solution.py:85
  139.5 10.6 %reshape.152 = bf16[7168,2,28]{2,1,0:T(2,128)(2,1)} reshape(bf16[8,2,25088]{2,1,0:T(2,128)(2,1)S(1)} %all_to_all.18) | data formatting | bytes 1605632
  150.1 9.9 %copy.54 = bf16[2,28,8,896]{3,0,1,2:T(2,128)(2,1)} copy(bf16[2,28,8,896]{1,0,3,2:T(2,128)(2,1)} %bitcast.96) | data formatting | bytes 1605632 | tf_op jit(solution)/shard_map/all_to_all | solution.py:85
  160.0 0.0 all-gather.12.cloned.1.call-update
  160.0 0.0 all-gather.10.cloned.1.call-start
  160.1 22.6 %reduce-scatter.3.cloned.1.call-done = bf16[48,3584]{1,0:T(8,128)(2,1)} async-done(((bf16[384,3584]{1,0:T(8,128)(2,1)}), bf16[48,3584]{1,0:T(8,128)(2,1)}) %reduce-scatter.3.cloned.1.call-update) | async-done | bytes 344080 | tf_op jit(solution)/shard_map/reduce_scatter | solution.py:76
  182.7 1.1 fusion.37
  183.9 1.3 multiply_reduce_fusion.1
  185.2 1.9 multiply_convert_fusion.1
  187.2 0.0 all-gather.10.cloned.1.call-update
  187.2 0.0 reduce-scatter.5.cloned.1.call-start
  187.2 70.7 %all-gather.12.cloned.1.call-done = bf16[2,3584,896]{2,0,1:T(2,128)(2,1)} async-done(((bf16[2,224,896]{2,0,1:T(2,128)(2,1)}), bf16[2,3584,896]{2,0,1:T(2,128)(2,1)}) %all-gather.12.cloned.1.call-update) | async-done | bytes 12845072 | tf_op jit(solution)/shard_map/all_gather | solution.py:86
  258.0 26.0 %fusion.46 = (bf16[1,3584,896]{2,0,1:T(2,128)(2,1)}, bf16[1,3584,896]{2,0,1:T(2,128)(2,1)}) fusion(bf16[2,3584,896]{2,0,1:T(2,128)(2,1)} %all-gather.12.cloned.1.call-done), kind=kLoop, calls=%fused_computation.58 | loop fusion | bytes 25690112 | tf_op jit(solution)/shard_map/slice | solution.py:87
  284.0 35.7 %all-gather.10.cloned.1.call-done = bf16[384,3584]{1,0:T(8,128)(2,1)} async-done(((bf16[48,3584]{1,0:T(8,128)(2,1)}), bf16[384,3584]{1,0:T(8,128)(2,1)}) %all-gather.10.cloned.1.call-update) | async-done | bytes 2752528 | tf_op jit(solution)/shard_map/all_gather | solution.py:83
  319.7 9.6 %fusion.9 = f32[384,896]{1,0:T(8,128)} fusion(bf16[384,3584]{1,0:T(8,128)(2,1)} %all-gather.10.cloned.1.call-done, bf16[1,3584,896]{2,0,1:T(2,128)(2,1)} %get-tuple-element.5), kind=kOutput, calls=%fused_computation.13 | convolution fusion | flops 2466250752 | bytes 10551296 | tf_op jit(solution)/shard_map/dot_general | solution.py:87
  329.3 15.2 %convolution_convert_fusion.1 = bf16[384,3584]{1,0:T(8,128)(2,1)} fusion(bf16[896,3584]{1,0:T(8,128)(2,1)} %param.16, bf16[384,3584]{1,0:T(8,128)(2,1)} %all-gather.10.cloned.1.call-done, bf16[1,3584,896]{2,0,1:T(2,128)(2,1)} %get-tuple-element.6, f32[384,896]{1,0:T(8,128)} %fusion.9), kind=kOutput, calls=%fused_computation.15 | convolution fusion | flops 4937318400 | bytes 19726336 | tf_op jit(solution)/shard_map/dot_general | solution.py:90
  344.5 0.0 reduce-scatter.5.cloned.1.call-update
  344.5 0.3 all-gather.14.cloned.1.call-start
  344.8 74.3 %reduce-scatter.5.cloned.1.call-done = bf16[48,3584]{1,0:T(8,128)(2,1)} async-done(((bf16[384,3584]{1,0:T(8,128)(2,1)}), bf16[48,3584]{1,0:T(8,128)(2,1)}) %reduce-scatter.5.cloned.1.call-update) | async-done | bytes 344080 | tf_op jit(solution)/shard_map/reduce_scatter | solution.py:76
  419.1 1.1 fusion.40
  420.3 1.4 multiply_reduce_fusion
  421.7 2.0 multiply_convert_fusion
  423.8 0.0 all-gather.14.cloned.1.call-update
  423.8 59.3 %all-gather.14.cloned.1.call-done = bf16[384,3584]{1,0:T(8,128)(2,1)} async-done(((bf16[48,3584]{1,0:T(8,128)(2,1)}), bf16[384,3584]{1,0:T(8,128)(2,1)}) %all-gather.14.cloned.1.call-update) | async-done | bytes 2752528 | tf_op jit(solution)/shard_map/all_gather | solution.py:93
  483.1 7.8 %convolution_convert_fusion.2 = bf16[384,1024]{1,0:T(8,128)(2,1)} fusion(bf16[384,3584]{1,0:T(8,128)(2,1)} %all-gather.14.cloned.1.call-done, bf16[3584,1024]{1,0:T(8,128)(2,1)} %param.17), kind=kOutput, calls=%fused_computation.22 | convolution fusion | flops 2818965504 | bytes 10878976 | tf_op jit(solution)/shard_map/dot_general | solution.py:94
  (23 shorter events, 0.1 us)
Async XLA Ops:
  6.5 42.2 %all-gather.6.cloned.1.call-start = ((), (), s32[]{:S(2)}) async-start(), calls=%async_computation.3 | async-start | bytes 3342336 | tf_op jit(solution)/shard_map/all_gather | solution.py:41
  8.3 78.1 %all-gather.8.cloned.1.call-start = ((), (), s32[]{:S(2)}) async-start(), calls=%async_computation.4 | async-start | bytes 3342336 | tf_op jit(solution)/shard_map/all_gather | solution.py:42
  9.1 173.6 %reduce-scatter.3.cloned.1.call-start = ((), (), s32[]{:S(2)}) async-start(), calls=%async_computation.5 | async-start | bytes 3096576 | tf_op jit(solution)/shard_map/reduce_scatter | solution.py:76
  54.2 6.5 %copy-start = (f32[6144,384,2]{1,0,2:T(8,128)}, f32[6144,384,2]{1,0,2:T(8,128)S(1)}, u32[]{:S(2)}) copy-start(f32[6144,384,2]{1,0,2:T(8,128)S(1)} %get-tuple-element.10) | copy-start | bytes 56623108
  86.5 13.2 %copy-start.2 = (bf16[512,3584]{1,0:T(8,128)(2,1)S(1)}, bf16[512,3584]{1,0:T(8,128)(2,1)}, u32[]{:S(2)}) copy-start(bf16[512,3584]{1,0:T(8,128)(2,1)} %param.14) | copy-start | bytes 11010052
  99.7 3.4 copy-start.3
  102.9 155.1 %all-gather.12.cloned.1.call-start = ((), (), s32[]{:S(2)}) async-start(), calls=%async_computation.7 | async-start | bytes 13647872 | tf_op jit(solution)/shard_map/all_gather | solution.py:86
  150.1 33.8 %copy-start.4 = (bf16[384,3584]{1,0:T(8,128)(2,1)S(1)}, bf16[384,3584]{1,0:T(8,128)(2,1)}, u32[]{:S(2)}) copy-start(bf16[384,3584]{1,0:T(8,128)(2,1)} %param.11) | copy-start | bytes 8257540
  150.1 33.8 %copy-start.5 = (f32[3584]{0:T(1024)S(1)}, f32[3584]{0:T(1024)}, u32[]{:S(2)}) copy-start(f32[3584]{0:T(1024)} %param.18) | copy-start | bytes 43012
  150.1 35.1 %copy-start.7 = (f32[3584]{0:T(1024)S(1)}, f32[3584]{0:T(1024)}, u32[]{:S(2)}) copy-start(f32[3584]{0:T(1024)} %param.19) | copy-start | bytes 43012
  160.0 159.7 %all-gather.10.cloned.1.call-start = ((), (), s32[]{:S(2)}) async-start(), calls=%async_computation.6 | async-start | bytes 3096576 | tf_op jit(solution)/shard_map/all_gather | solution.py:83
  187.2 231.9 %reduce-scatter.5.cloned.1.call-start = ((), (), s32[]{:S(2)}) async-start(), calls=%async_computation.8 | async-start | bytes 3096576 | tf_op jit(solution)/shard_map/reduce_scatter | solution.py:76
  329.3 91.0 %copy-start.1 = (bf16[48,3584]{1,0:T(8,128)(2,1)S(1)}, bf16[48,3584]{1,0:T(8,128)(2,1)}, u32[]{:S(2)}) copy-start(bf16[48,3584]{1,0:T(8,128)(2,1)} %reduce-scatter.3.cloned.1.call-done) | copy-start | bytes 1032196
  329.3 91.0 %copy-start.6 = (f32[3584]{0:T(1024)S(1)}, f32[3584]{0:T(1024)}, u32[]{:S(2)}) copy-start(f32[3584]{0:T(1024)} %param.20) | copy-start | bytes 43012
  344.5 77.2 %copy-start.8 = (f32[3584]{0:T(1024)S(1)}, f32[3584]{0:T(1024)}, u32[]{:S(2)}) copy-start(f32[3584]{0:T(1024)} %param.21) | copy-start | bytes 43012
  344.5 138.5 %all-gather.14.cloned.1.call-start = ((), (), s32[]{:S(2)}) async-start(), calls=%async_computation.9 | async-start | bytes 3096576 | tf_op jit(solution)/shard_map/all_gather | solution.py:93
Sparse Core Ops, SparseCore 0:
  9.1 39.6 all-gather.5
  50.5 35.9 all-gather.7
  103.0 79.6 reduce-scatter.2
  184.3 73.6 all-gather.11
  260.1 59.5 all-gather.9
  344.6 74.4 reduce-scatter.4
  423.9 59.1 all-gather.13
where the time goes:
time: 498 us
  waiting for transfers between devices  317 us (64%)
  local copies, waits for them, and re-layouts  71 us (14%)
  matrix products  54.3 us (11%)
  blocking collectives  21.5 us (4%)
  other arithmetic  19.9 us (4%)
  between operations  13.7 us (3%)
    reduce_scatter x2, waiting for transfers between devices, scattered(): lax.psum_scatter(values.astype(jnp.bfloat16), 'tp', scatter_dimension=0,...  96.9 us
    all_gather x1, waiting for transfers between devices, local(): local_units = lax.all_gather(unit_rows, 'seq', axis=1, tiled=True)  70.7 us
    all_gather x1, waiting for transfers between devices, local(): next_in = lax.all_gather(next_in, 'tp', axis=0, tiled=True)  59.3 us
    all_gather x1, waiting for transfers between devices, local(): ffw_in = lax.all_gather(ffw_in, 'tp', axis=0, tiled=True)  35.7 us
    all_gather x1, waiting for transfers between devices, local(): lax.all_gather(own_keys, 'seq', axis=0, tiled=True)  33.6 us
    slice x1, local copies, waits for them, and re-layouts, local(): gate = jnp.dot(ffw_in, local_units[0], preferred_element_type=jnp.float32)  26 us
    unnamed x21, local copies, waits for them, and re-layouts  25.8 us
    all_to_all x1, blocking collectives, local(): lax.all_to_all(server_low, 'tp', split_axis=2, concat_axis=1, tiled=True)  21.5 us
  transfers between devices with their start and end apart: 7, of which 7 were waited for; matrix products, arithmetic and copies ran while one was open for 17% of the time, Pallas kernels for 0%

commit v1 on v0

--- a/solution.py
+++ b/solution.py
@@ -6,6 +6,11 @@
 HEADS = 16
 KV_HEADS = 8
 HEAD_DIM = 256
+
+
+def exchange_gather(block, axis, along):
+    sent = jnp.stack([block] * lax.axis_size(axis))
+    return jnp.concatenate(lax.all_to_all(sent, axis, 0, 0), axis=along)
 
 
 def rms_norm(values, gain):
@@ -90,7 +95,7 @@
     ffw_out = jnp.dot(activated, down_weight, preferred_element_type=jnp.float32)
     residual_out = residual_mid + rms_norm(scattered(ffw_out), post_ffw_gain)
     next_in = rms_norm(residual_out, next_gain).astype(jnp.bfloat16)
-    next_in = lax.all_gather(next_in, "tp", axis=0, tiled=True)
+    next_in = exchange_gather(next_in, "tp", 0)
     return jnp.dot(next_in, next_weight, preferred_element_type=jnp.float32).astype(jnp.bfloat16)
 
 

time: 498 us -> 476 us (0.956)
  waiting for transfers between devices: 317 us -> 258 us
  blocking collectives: 21.5 us -> 57.6 us
    all_gather x1 -> x0, waiting for transfers between devices: 59.3 us -> none  [local(): next_in = lax.all_gather(next_in, 'tp', axis=0, tiled=True)]
    all_to_all x0 -> x1, blocking collectives: none -> 36.1 us  [exchange_gather(): return jnp.concatenate(lax.all_to_all(sent, axis, 0, 0), axis=along)]
  transfers between devices with their start and end apart: 7 -> 6, of which waited for: 7 -> 6; matrix products, arithmetic and copies ran while one was open for 17% -> 18% of each run, Pallas kernels for 0% -> 0%
where the time goes in v1:
time: 476 us; the launch traced here: 473 us
  waiting for transfers between devices  258 us (54%)
  local copies, waits for them, and re-layouts  71.2 us (15%)
  blocking collectives  57.6 us (12%)
  matrix products  53.6 us (11%)
  other arithmetic  19.2 us (4%)
  between operations  13.7 us (3%)
    reduce_scatter x2, waiting for transfers between devices, scattered(): lax.psum_scatter(values.astype(jnp.bfloat16), 'tp', scatter_dimension=0,...  97.2 us
    all_gather x1, waiting for transfers between devices, local(): local_units = lax.all_gather(unit_rows, 'seq', axis=1, tiled=True)  70.7 us
    all_to_all x1, blocking collectives, exchange_gather(): return jnp.concatenate(lax.all_to_all(sent, axis, 0, 0), axis=along)  36.1 us
    all_gather x1, waiting for transfers between devices, local(): ffw_in = lax.all_gather(ffw_in, 'tp', axis=0, tiled=True)  35.7 us
    all_gather x1, waiting for transfers between devices, local(): lax.all_gather(own_keys, 'seq', axis=0, tiled=True)  33.6 us
    slice x1, local copies, waits for them, and re-layouts, local(): gate = jnp.dot(ffw_in, local_units[0], preferred_element_type=jnp.float32)  26 us
    unnamed x21, local copies, waits for them, and re-layouts  25.8 us
    all_to_all x1, blocking collectives, local(): lax.all_to_all(server_low, 'tp', split_axis=2, concat_axis=1, tiled=True)  21.5 us
  transfers between devices with their start and end apart: 6, of which 6 were waited for; matrix products, arithmetic and copies ran while one was open for 18% of the time, Pallas kernels for 0%

profile of v1, /device:TPU:1, one launch (start us, length us, event | category | flops | bytes accessed | tf_op | source)
XLA Modules:
  0.0 473.3 jit_solution(14009299254812418653)
XLA Ops:
  6.5 1.8 fusion.47
  8.3 0.0 all-gather.5.cloned.1.call-update
  8.3 0.0 all-gather.7.cloned.1.call-start
  8.4 0.7 all-gather.7.cloned.1.call-update
  9.1 0.0 reduce-scatter.3.cloned.1.call-start
  9.1 1.0 slice.21
  10.2 0.8 reduce-window.8
  11.0 0.2 copy.48
  11.2 0.1 convert_reduce_fusion
  11.4 0.1 dynamic_slice.7
  11.4 3.8 fusion.6
  15.2 33.6 %all-gather.5.cloned.1.call-done = bf16[6144,1,256]{2,0,1:T(8,128)(2,1)} async-done(((bf16[384,1,256]{2,0,1:T(8,128)(2,1)}), bf16[6144,1,256]{2,0,1:T(8,128)(2,1)}) %all-gather.5.cloned.1.call-update) | async-done | bytes 3145744 | tf_op jit(solution)/shard_map/all_gather | solution.py:46
  48.8 5.4 %fusion = (f32[384,2]{0,1:T(2,128)S(1)}, f32[6144,384,2]{1,0,2:T(8,128)S(1)}) fusion(pred[384,6144]{0,1:T(8,128)(4,1)} %fusion.6, bf16[384,2,256]{0,2,1:T(8,128)(2,1)S(1)} %bitcast.102, bf16[6144,1,256]{2,0,1:T(8,128)(2,1)} %all-gather.5.cloned.1.call-done), kind=kOutput, calls=%fused_computation.2 | convolution fusion | flops 2430074112 | bytes 24775680 | tf_op jit(solution)/shard_map/qgrd,kgd->qgrk/dot_general | solution.py:59
  54.2 6.5 %copy-done = f32[6144,384,2]{1,0,2:T(8,128)} copy-done((f32[6144,384,2]{1,0,2:T(8,128)}, f32[6144,384,2]{1,0,2:T(8,128)S(1)}, u32[]{:S(2)}) %copy-start) | copy-done | bytes 18874392
  60.7 6.1 %fusion.1 = f32[384,2]{0,1:T(2,128)S(1)} fusion(f32[6144,384,2]{1,0,2:T(8,128)S(1)} %get-tuple-element.10, f32[384,2]{0,1:T(2,128)S(1)} %get-tuple-element.9, pred[384,6144]{0,1:T(8,128)(4,1)} %fusion.6), kind=kLoop, calls=%fused_computation.3 | loop fusion | flops 23592192 | bytes 21239808 | tf_op jit(solution)/shard_map/reduce_sum | solution.py:67
  66.8 19.6 %all-gather.7.cloned.1.call-done = bf16[6144,1,256]{2,0,1:T(8,128)(2,1)} async-done(((bf16[384,1,256]{2,0,1:T(8,128)(2,1)}), bf16[6144,1,256]{2,0,1:T(8,128)(2,1)}) %all-gather.7.cloned.1.call-update) | async-done | bytes 3145744 | tf_op jit(solution)/shard_map/all_gather | solution.py:47
  86.5 13.2 %fusion.32 = bf16[1,256,384,2]{2,1,3,0:T(8,128)(2,1)S(1)} fusion(bf16[6144,1,256]{2,0,1:T(8,128)(2,1)} %all-gather.7.cloned.1.call-done, f32[6144,384,2]{1,0,2:T(8,128)} %copy-done, f32[384,2]{0,1:T(2,128)S(1)} %get-tuple-element.9, pred[384,6144]{0,1:T(8,128)(4,1)} %fusion.6, f32[384,2]{0,1:T(2,128)S(1)} %fusion.1), kind=kOutput, calls=%fused_computation.33 | convolution fusion | flops 2439905280 | bytes 24778752 | tf_op jit(solution)/shard_map/qgrk,kgd->qgrd/dot_general | solution.py:68
  99.7 0.0 copy-start.3
  99.7 3.1 convolution_convert_fusion
  102.8 0.0 reduce-scatter.3.cloned.1.call-update
  102.8 0.2 all-gather.11.cloned.1.call-start
  103.1 0.5 copy.72
  103.6 6.2 %copy.53 = bf16[2,28,7168]{1,0,2:T(2,128)(2,1)} copy(bf16[2,28,7168]{2,1,0:T(8,128)(2,1)S(1)} %copy.72) | data formatting | bytes 1605632 | tf_op jit(solution)/shard_map/convert_element_type | solution.py:89
  109.7 8.3 %reshape.157 = bf16[8,2,25088]{2,1,0:T(2,128)(2,1)S(1)} reshape(bf16[7168,2,28]{2,1,0:T(2,128)(2,1)} %bitcast.96) | data formatting | bytes 1605632
  118.0 21.5 %all_to_all.23 = bf16[8,2,25088]{2,1,0:T(2,128)(2,1)S(1)} all-to-all(bf16[8,2,25088]{2,1,0:T(2,128)(2,1)S(1)} %reshape.157), channel_id=1, replica_groups=mesh['seq'=16,'tp'=8] {'tp'}, dimensions={0} | all-to-all | bytes 1605632 | tf_op jit(solution)/shard_map/all_to_all | solution.py:90
  139.5 10.6 %reshape.158 = bf16[7168,2,28]{2,1,0:T(2,128)(2,1)} reshape(bf16[8,2,25088]{2,1,0:T(2,128)(2,1)S(1)} %all_to_all.23) | data formatting | bytes 1605632
  150.1 9.9 %copy.54 = bf16[2,28,8,896]{3,0,1,2:T(2,128)(2,1)} copy(bf16[2,28,8,896]{1,0,3,2:T(2,128)(2,1)} %bitcast.97) | data formatting | bytes 1605632 | tf_op jit(solution)/shard_map/all_to_all | solution.py:90
  160.0 0.0 all-gather.11.cloned.1.call-update
  160.0 0.0 all-gather.9.cloned.1.call-start
  160.1 22.6 %reduce-scatter.3.cloned.1.call-done = bf16[48,3584]{1,0:T(8,128)(2,1)} async-done(((bf16[384,3584]{1,0:T(8,128)(2,1)}), bf16[48,3584]{1,0:T(8,128)(2,1)}) %reduce-scatter.3.cloned.1.call-update) | async-done | bytes 344080 | tf_op jit(solution)/shard_map/reduce_scatter | solution.py:81
  182.7 1.1 fusion.37
  183.9 1.3 multiply_reduce_fusion.1
  185.2 1.9 multiply_convert_fusion.1
  187.1 0.0 all-gather.9.cloned.1.call-update
  187.2 0.0 reduce-scatter.5.cloned.1.call-start
  187.2 70.7 %all-gather.11.cloned.1.call-done = bf16[2,3584,896]{2,0,1:T(2,128)(2,1)} async-done(((bf16[2,224,896]{2,0,1:T(2,128)(2,1)}), bf16[2,3584,896]{2,0,1:T(2,128)(2,1)}) %all-gather.11.cloned.1.call-update) | async-done | bytes 12845072 | tf_op jit(solution)/shard_map/all_gather | solution.py:91
  258.0 26.0 %fusion.46 = (bf16[1,3584,896]{2,0,1:T(2,128)(2,1)}, bf16[1,3584,896]{2,0,1:T(2,128)(2,1)}) fusion(bf16[2,3584,896]{2,0,1:T(2,128)(2,1)} %all-gather.11.cloned.1.call-done), kind=kLoop, calls=%fused_computation.58 | loop fusion | bytes 25690112 | tf_op jit(solution)/shard_map/slice | solution.py:92
  283.9 35.7 %all-gather.9.cloned.1.call-done = bf16[384,3584]{1,0:T(8,128)(2,1)} async-done(((bf16[48,3584]{1,0:T(8,128)(2,1)}), bf16[384,3584]{1,0:T(8,128)(2,1)}) %all-gather.9.cloned.1.call-update) | async-done | bytes 2752528 | tf_op jit(solution)/shard_map/all_gather | solution.py:88
  319.7 9.6 %fusion.9 = f32[384,896]{1,0:T(8,128)} fusion(bf16[384,3584]{1,0:T(8,128)(2,1)} %all-gather.9.cloned.1.call-done, bf16[1,3584,896]{2,0,1:T(2,128)(2,1)} %get-tuple-element.5), kind=kOutput, calls=%fused_computation.13 | convolution fusion | flops 2466250752 | bytes 10551296 | tf_op jit(solution)/shard_map/dot_general | solution.py:92
  329.3 15.2 %convolution_convert_fusion.1 = bf16[384,3584]{1,0:T(8,128)(2,1)} fusion(bf16[896,3584]{1,0:T(8,128)(2,1)} %param.16, bf16[384,3584]{1,0:T(8,128)(2,1)} %all-gather.9.cloned.1.call-done, bf16[1,3584,896]{2,0,1:T(2,128)(2,1)} %get-tuple-element.6, f32[384,896]{1,0:T(8,128)} %fusion.9), kind=kOutput, calls=%fused_computation.15 | convolution fusion | flops 4937318400 | bytes 19726336 | tf_op jit(solution)/shard_map/dot_general | solution.py:95
  344.5 0.0 reduce-scatter.5.cloned.1.call-update
  344.5 74.6 %reduce-scatter.5.cloned.1.call-done = bf16[48,3584]{1,0:T(8,128)(2,1)} async-done(((bf16[384,3584]{1,0:T(8,128)(2,1)}), bf16[48,3584]{1,0:T(8,128)(2,1)}) %reduce-scatter.5.cloned.1.call-update) | async-done | bytes 344080 | tf_op jit(solution)/shard_map/reduce_scatter | solution.py:81
  419.1 1.1 fusion.40
  420.3 1.4 multiply_reduce_fusion
  421.7 1.3 multiply_convert_fusion
  423.0 0.2 stack.2
  423.2 36.1 %all_to_all.24 = bf16[8,48,3584]{2,1,0:T(8,128)(2,1)S(1)} all-to-all(bf16[8,48,3584]{2,1,0:T(8,128)(2,1)S(1)} %stack.2), channel_id=1, replica_groups=mesh['seq'=16,'tp'=8] {'tp'}, dimensions={0} | all-to-all | bytes 5505024 | tf_op jit(solution)/shard_map/all_to_all | solution.py:13
  459.3 7.1 %convolution_convert_fusion.2 = bf16[384,1024]{1,0:T(8,128)(2,1)} fusion(bf16[384,3584]{1,0:T(8,128)(2,1)S(1)} %bitcast.99, bf16[3584,1024]{1,0:T(8,128)(2,1)} %param.17), kind=kOutput, calls=%fused_computation.22 | convolution fusion | flops 2818965504 | bytes 10878976 | tf_op jit(solution)/shard_map/dot_general | solution.py:99
  (22 shorter events, 0.1 us)
Async XLA Ops:
  6.5 42.2 %all-gather.5.cloned.1.call-start = ((), (), s32[]{:S(2)}) async-start(), calls=%async_computation.4 | async-start | bytes 3342336 | tf_op jit(solution)/shard_map/all_gather | solution.py:46
  8.3 78.1 %all-gather.7.cloned.1.call-start = ((), (), s32[]{:S(2)}) async-start(), calls=%async_computation.5 | async-start | bytes 3342336 | tf_op jit(solution)/shard_map/all_gather | solution.py:47
  9.1 173.6 %reduce-scatter.3.cloned.1.call-start = ((), (), s32[]{:S(2)}) async-start(), calls=%async_computation.6 | async-start | bytes 3096576 | tf_op jit(solution)/shard_map/reduce_scatter | solution.py:81
  54.2 6.5 %copy-start = (f32[6144,384,2]{1,0,2:T(8,128)}, f32[6144,384,2]{1,0,2:T(8,128)S(1)}, u32[]{:S(2)}) copy-start(f32[6144,384,2]{1,0,2:T(8,128)S(1)} %get-tuple-element.10) | copy-start | bytes 56623108
  86.5 13.2 %copy-start.2 = (bf16[512,3584]{1,0:T(8,128)(2,1)S(1)}, bf16[512,3584]{1,0:T(8,128)(2,1)}, u32[]{:S(2)}) copy-start(bf16[512,3584]{1,0:T(8,128)(2,1)} %param.14) | copy-start | bytes 11010052
  99.7 3.4 copy-start.3
  102.8 155.1 %all-gather.11.cloned.1.call-start = ((), (), s32[]{:S(2)}) async-start(), calls=%async_computation.8 | async-start | bytes 13647872 | tf_op jit(solution)/shard_map/all_gather | solution.py:91
  150.1 33.7 %copy-start.4 = (bf16[384,3584]{1,0:T(8,128)(2,1)S(1)}, bf16[384,3584]{1,0:T(8,128)(2,1)}, u32[]{:S(2)}) copy-start(bf16[384,3584]{1,0:T(8,128)(2,1)} %param.11) | copy-start | bytes 8257540
  150.1 33.7 %copy-start.5 = (f32[3584]{0:T(1024)S(1)}, f32[3584]{0:T(1024)}, u32[]{:S(2)}) copy-start(f32[3584]{0:T(1024)} %param.18) | copy-start | bytes 43012
  150.1 35.1 %copy-start.7 = (f32[3584]{0:T(1024)S(1)}, f32[3584]{0:T(1024)}, u32[]{:S(2)}) copy-start(f32[3584]{0:T(1024)} %param.19) | copy-start | bytes 43012
  160.0 159.7 %all-gather.9.cloned.1.call-start = ((), (), s32[]{:S(2)}) async-start(), calls=%async_computation.7 | async-start | bytes 3096576 | tf_op jit(solution)/shard_map/all_gather | solution.py:88
  187.2 231.9 %reduce-scatter.5.cloned.1.call-start = ((), (), s32[]{:S(2)}) async-start(), calls=%async_computation.9 | async-start | bytes 3096576 | tf_op jit(solution)/shard_map/reduce_scatter | solution.py:81
  329.3 91.0 %copy-start.1 = (bf16[48,3584]{1,0:T(8,128)(2,1)S(1)}, bf16[48,3584]{1,0:T(8,128)(2,1)}, u32[]{:S(2)}) copy-start(bf16[48,3584]{1,0:T(8,128)(2,1)} %reduce-scatter.3.cloned.1.call-done) | copy-start | bytes 1032196
  329.3 91.0 %copy-start.6 = (f32[3584]{0:T(1024)S(1)}, f32[3584]{0:T(1024)}, u32[]{:S(2)}) copy-start(f32[3584]{0:T(1024)} %param.20) | copy-start | bytes 43012
  344.5 77.2 %copy-start.8 = (f32[3584]{0:T(1024)S(1)}, f32[3584]{0:T(1024)}, u32[]{:S(2)}) copy-start(f32[3584]{0:T(1024)} %param.21) | copy-start | bytes 43012
Sparse Core Ops, SparseCore 0:
  9.1 39.6 all-gather.4
  50.5 35.9 all-gather.6
  103.0 79.6 reduce-scatter.2
  184.2 73.6 all-gather.10
  260.1 59.5 all-gather.8
  344.6 74.4 reduce-scatter.4
